TPU v7x, 256 devices: a whole 4x4x8 slice. The times are simulated.
256 devices in a mesh: pipe: 16 (over z, core), dp: 4 (over x), tensor: 4 (over y).
Axes of the slice: x: 4, y: 4, z: 8, core: 2. Of those that a mesh axis runs over, the one named last changes fastest.
Arguments:
- acts: bfloat16 [16, 2048, 8192], P('pipe', 'dp', 'tensor'), may hold values from -6 to 6
- grads: bfloat16 [16, 2048, 8192], P('pipe', 'dp', 'tensor'), may hold values from -6 to 6
- sketch_index: int32 [16, 2, 16], P('pipe'), may hold values from 0 to 63, as said below
- sketch_values: bfloat16 [16, 2, 16, 128, 32], P('pipe'), may hold values from -0.125 to 0.125
Outputs:
- basis: float32 [16384, 256], P(('pipe', 'tensor'), 'dp')
Inputs may be any that keep to these rules, and one draw needn't show every extreme that they name: `sketch_index`: the 16 blocks of each sketch are distinct.
All inputs are finite; a program needn't handle non-finite values.
Results may differ from a plain program's by a relative error of at most 0.0003.
Values sent between devices are 32-bit elements; how exact they have to be, the bound alone decides.
A program may use at most 64 MiB of HBM per device.

v0:
```python
import jax
import jax.numpy as jnp
from jax import lax
from jax.sharding import PartitionSpec as P

RANK = 256
ITERS = 2
TOK_EX = 4


def mm(a, b):
    return jnp.matmul(a, b, precision=lax.Precision.HIGHEST)


def mm_tn(a, b):
    return lax.dot_general(a, b, (((0,), (0,)), ((), ())), precision=lax.Precision.HIGHEST)


def solve_lower_t(lower, block):
    return lax.linalg.triangular_solve(lower, block, left_side=False, lower=True, transpose_a=True)


def merged_coords(gram):
    cols = gram.shape[0]
    eye = jnp.eye(RANK, dtype=gram.dtype)
    pick = jnp.concatenate([eye] * (cols // RANK), axis=0)
    lower = jnp.linalg.cholesky(mm_tn(pick, mm(gram, pick)))
    coords = solve_lower_t(lower, pick)
    for turn in range(ITERS):
        image = mm(gram, coords)
        lower = jnp.linalg.cholesky(mm_tn(image, mm(gram, image)))
        coords = solve_lower_t(lower, image)
    weights = mm(gram, coords)
    lower = jnp.linalg.cholesky(mm_tn(weights, weights))
    return mm(coords, lower)


def shards(acts, grads, sketch_index, sketch_values):
    local_width = acts.shape[2]
    blocks = local_width // 128
    width = sketch_values.shape[4]
    tensor_pos = lax.axis_index("tensor")
    tensor_count = lax.axis_size("tensor")
    dp_pos = lax.axis_index("dp")
    dp_count = lax.axis_size("dp")
    span = jnp.arange(blocks, dtype=jnp.int32) + tensor_pos * blocks
    onehot = (sketch_index[0][:, :, None] == span[None, None, :]).astype(jnp.bfloat16)
    local = jnp.einsum(
        "sij,sicd->sjcd", onehot, sketch_values[0], preferred_element_type=jnp.float32
    )
    local = local.astype(jnp.bfloat16).reshape(2, local_width, width)
    left_part = jnp.dot(acts[0], local[0], preferred_element_type=jnp.float32)
    right_part = jnp.dot(grads[0], local[1], preferred_element_type=jnp.float32)
    both = lax.psum(jnp.concatenate([left_part, right_part], axis=1), "tensor")
    both = lax.all_gather(both, "dp", axis=0, tiled=True)
    left_all = both[:, :width].reshape(-1, TOK_EX, width)
    right_all = both[:, width:].reshape(-1, TOK_EX, width)
    outer = jnp.einsum("etk,etl->ekl", left_all, right_all, precision=lax.Precision.HIGHEST)
    joined_t = outer.reshape(outer.shape[0], -1)
    gram = lax.psum(mm(joined_t, joined_t.T), "pipe")
    coords = merged_coords(gram)
    part_rows = joined_t.shape[1] // tensor_count
    rows = lax.dynamic_slice_in_dim(joined_t, tensor_pos * part_rows, part_rows, 1)
    own_columns = coords.shape[1] // dp_count
    coords = lax.dynamic_slice_in_dim(coords, dp_pos * own_columns, own_columns, 1)
    return mm_tn(rows, coords)


def solution(mesh):
    placed = (
        P("pipe", "dp", "tensor"),
        P("pipe", "dp", "tensor"),
        P("pipe", None, None),
        P("pipe", None, None, None, None),
    )
    return jax.shard_map(
        shards, mesh=mesh, in_specs=placed, out_specs=P(("pipe", "tensor"), "dp"), check_vma=False
    )
```

profile of v0, /device:TPU:1, one launch (start us, length us, event | category | flops | bytes accessed | tf_op | source)
XLA Modules:
  0.0 487.8 jit_solution(8322790528402684456)
XLA Ops:
  6.5 1.4 convolution_convert_fusion
  10.4 48.4 %all-reduce.4.cloned.1.call-done = f32[512,64]{0,1:T(8,128)} async-done(((f32[512,64]{0,1:T(8,128)}), f32[512,64]{0,1:T(8,128)}) %all-reduce.4.cloned.1.call-update) | async-done | bytes 131088 | tf_op jit(solution)/shard_map/psum | solution.py:54
  58.8 10.5 %all_gather.3 = f32[2048,64]{0,1:T(8,128)S(1)} all-gather(f32[512,64]{0,1:T(8,128)} %all-reduce.4.cloned.1.call-done), channel_id=1, replica_groups=mesh['pipe'=16,'dp'=4,'tensor'=4] {'dp'}, dimensions={0}, use_global_device_ids=true | all-gather | bytes 655360 | tf_op jit(solution)/shard_map/all_gather | solution.py:55
  70.1 1.3 copy.15
  71.4 1.4 copy.16
  72.8 16.5 %fusion.90 = f32[512,32,32]{2,1,0:T(8,128)} fusion(f32[512,4,32]{2,1,0:T(4,128)S(1)} %bitcast.168, f32[512,4,32]{2,1,0:T(4,128)} %bitcast.169), kind=kOutput, calls=%fused_computation.147 | convolution fusion | flops 25165824 | bytes 2621440 | tf_op jit(solution)/shard_map/etk,etl->ekl/dot_general | solution.py:58
  89.2 6.4 %copy.17 = f32[512,32,32]{0,2,1:T(8,128)} copy(f32[512,32,32]{2,1,0:T(8,128)} %fusion.90) | data formatting | bytes 4194304 | tf_op jit(solution)/shard_map/etk,etl->ekl/dot_general | solution.py:58
  95.7 6.8 %convolution_bitcast_fusion = f32[512,512]{1,0:T(8,128)} fusion(f32[512,32,32]{0,2,1:T(8,128)} %copy.17), kind=kOutput, calls=%fused_computation.10 | convolution fusion | flops 3221225472 | bytes 3145728 | tf_op jit(solution)/shard_map/dot_general | solution.py:12
  102.5 0.8 fusion.71
  103.4 116.2 %all-reduce.6.cloned.1.call-done = f32[512,512]{1,0:T(8,128)} async-done(((f32[512,512]{1,0:T(8,128)}), f32[512,512]{1,0:T(8,128)}) %all-reduce.6.cloned.1.call-update) | async-done | bytes 1048592 | tf_op jit(solution)/shard_map/psum | solution.py:60
  219.6 1.8 fusion.70
  223.0 11.7 %cholesky.214 = f32[128,128]{1,0:T(8,128)S(1)} custom-call(f32[128,128]{1,0:T(8,128)S(1)} %cholesky.346), custom_call_target="Cholesky" | custom-call | tf_op jit(solution)/shard_map/jit(cholesky)/cholesky | solution.py:27
  234.7 9.8 %custom-call.16 = f32[1,128,128]{1,2,0:T(8,128)S(1)} custom-call(f32[1,128,128]{2,1,0:T(8,128)S(1)} %get-tuple-element.79), custom_call_target="InvertDiagBlocksLowerTriangular" | custom-call | tf_op jit(solution)/shard_map/jit(cholesky)/cholesky | solution.py:27
  244.6 1.1 constant_dynamic-update-slice_fusion.7
  245.7 1.1 convolution_subtract_fusion.6
  246.8 12.1 %cholesky.231 = f32[128,128]{1,0:T(8,128)S(1)} custom-call(f32[128,128]{1,0:T(8,128)S(1)} %convolution_subtract_fusion.6), custom_call_target="Cholesky" | custom-call | tf_op jit(solution)/shard_map/jit(cholesky)/cholesky | solution.py:27
  260.9 1.0 select_select_fusion.2
  262.0 4.1 while.6
  262.7 1.3 bitcast_dynamic-update-slice_fusion.6
  264.7 1.3 bitcast_dynamic-update-slice_fusion.6
  266.7 20.5 %custom-call.17 = f32[2,128,128]{1,2,0:T(8,128)S(1)} custom-call(f32[2,128,128]{2,1,0:T(8,128)} %copy-done.14), custom_call_target="InvertDiagBlocksLowerTriangular" | custom-call | tf_op jit(solution)/shard_map/triangular_solve/custom-call.0 | solution.py:20
  287.2 1.4 fusion.26
  288.6 1.5 convolution_subtract_fusion.2
  290.6 1.0 fusion.10
  291.6 1.0 fusion.91
  292.6 1.0 fusion.92
  293.6 0.8 copy.21
  294.5 1.0 fusion.30
  296.2 11.7 %cholesky.248 = f32[128,128]{1,0:T(8,128)S(1)} custom-call(f32[128,128]{1,0:T(8,128)S(1)} %cholesky.349), custom_call_target="Cholesky" | custom-call | tf_op jit(solution)/shard_map/jit(cholesky)/cholesky | solution.py:31
  307.9 9.8 %custom-call.18 = f32[1,128,128]{1,2,0:T(8,128)S(1)} custom-call(f32[1,128,128]{2,1,0:T(8,128)S(1)} %get-tuple-element.75), custom_call_target="InvertDiagBlocksLowerTriangular" | custom-call | tf_op jit(solution)/shard_map/jit(cholesky)/cholesky | solution.py:31
  317.7 1.0 constant_dynamic-update-slice_fusion.5
  318.8 1.1 convolution_subtract_fusion.5
  319.9 11.9 %cholesky.265 = f32[128,128]{1,0:T(8,128)S(1)} custom-call(f32[128,128]{1,0:T(8,128)S(1)} %convolution_subtract_fusion.5), custom_call_target="Cholesky" | custom-call | tf_op jit(solution)/shard_map/jit(cholesky)/cholesky | solution.py:31
  334.4 1.0 select_select_fusion.1
  335.4 4.1 while.7
  336.1 1.4 bitcast_dynamic-update-slice_fusion.7
  338.1 1.4 bitcast_dynamic-update-slice_fusion.7
  340.2 20.5 %custom-call.19 = f32[2,128,128]{1,2,0:T(8,128)S(1)} custom-call(f32[2,128,128]{2,1,0:T(8,128)} %copy-done.15), custom_call_target="InvertDiagBlocksLowerTriangular" | custom-call | tf_op jit(solution)/shard_map/triangular_solve/custom-call.0 | solution.py:20
  360.7 1.4 fusion.24
  362.1 1.5 convolution_subtract_fusion.1
  364.1 1.0 fusion.14
  365.1 1.0 fusion.93
  366.1 1.0 fusion.94
  367.1 0.8 copy.22
  367.9 1.0 fusion.29
  369.6 11.7 %cholesky.282 = f32[128,128]{1,0:T(8,128)S(1)} custom-call(f32[128,128]{1,0:T(8,128)S(1)} %cholesky.352), custom_call_target="Cholesky" | custom-call | tf_op jit(solution)/shard_map/jit(cholesky)/cholesky | solution.py:31
  381.4 9.8 %custom-call.20 = f32[1,128,128]{1,2,0:T(8,128)S(1)} custom-call(f32[1,128,128]{2,1,0:T(8,128)S(1)} %get-tuple-element.71), custom_call_target="InvertDiagBlocksLowerTriangular" | custom-call | tf_op jit(solution)/shard_map/jit(cholesky)/cholesky | solution.py:31
  391.2 1.0 constant_dynamic-update-slice_fusion.2
  392.3 1.1 convolution_subtract_fusion.4
  393.4 12.1 %cholesky.299 = f32[128,128]{1,0:T(8,128)S(1)} custom-call(f32[128,128]{1,0:T(8,128)S(1)} %convolution_subtract_fusion.4), custom_call_target="Cholesky" | custom-call | tf_op jit(solution)/shard_map/jit(cholesky)/cholesky | solution.py:31
  408.1 1.0 select_select_fusion
  409.2 4.1 while.8
  409.8 1.4 bitcast_dynamic-update-slice_fusion.8
  411.8 1.4 bitcast_dynamic-update-slice_fusion.8
  414.6 20.5 %custom-call.21 = f32[2,128,128]{1,2,0:T(8,128)S(1)} custom-call(f32[2,128,128]{2,1,0:T(8,128)} %copy-done.16), custom_call_target="InvertDiagBlocksLowerTriangular" | custom-call | tf_op jit(solution)/shard_map/triangular_solve/custom-call.0 | solution.py:20
  435.1 1.4 fusion.22
  436.5 1.6 convolution_subtract_fusion
  438.5 1.0 fusion.21
  439.6 1.0 fusion.95
  440.8 11.7 %cholesky.316 = f32[128,128]{1,0:T(8,128)S(1)} custom-call(f32[128,128]{1,0:T(8,128)S(1)} %cholesky.355), custom_call_target="Cholesky" | custom-call | tf_op jit(solution)/shard_map/jit(cholesky)/cholesky | solution.py:34
  452.6 9.8 %custom-call.22 = f32[1,128,128]{1,2,0:T(8,128)S(1)} custom-call(f32[1,128,128]{2,1,0:T(8,128)S(1)} %get-tuple-element.67), custom_call_target="InvertDiagBlocksLowerTriangular" | custom-call | tf_op jit(solution)/shard_map/jit(cholesky)/cholesky | solution.py:34
  462.9 11.9 %cholesky.333 = f32[128,128]{1,0:T(8,128)S(1)} custom-call(f32[128,128]{1,0:T(8,128)S(1)} %convolution_subtract_fusion.3), custom_call_target="Cholesky" | custom-call | tf_op jit(solution)/shard_map/jit(cholesky)/cholesky | solution.py:34
  477.4 1.0 fusion.20
  478.4 2.4 fusion.18
  (95 shorter events, 19.5 us)
Async XLA Ops:
  6.5 1.7 copy-start
  6.5 52.3 %all-reduce.4.cloned.1.call-start = ((), (), s32[]{:S(2)}) async-start(), calls=%async_computation | async-start | bytes 262144 | tf_op jit(solution)/shard_map/psum | solution.py:54
  6.5 2.4 copy-start.6
  10.4 209.2 %all-reduce.6.cloned.1.call-start = ((), (), s32[]{:S(2)}) async-start(), calls=%async_computation.1 | async-start | bytes 2097152 | tf_op jit(solution)/shard_map/psum | solution.py:60
  222.3 0.7 copy-start.11
  244.6 46.0 %copy-start.1 = (f32[512,512]{1,0:T(8,128)S(1)}, f32[512,512]{1,0:T(8,128)}, u32[]{:S(2)}) copy-start(f32[512,512]{1,0:T(8,128)} %all-reduce.6.cloned.1.call-done) | copy-start | bytes 3145732
  259.0 1.9 copy-start.10
  266.1 0.6 copy-start.14
  291.6 1.0 copy-start.3
  295.4 0.7 copy-start.12
  331.8 2.6 copy-start.8
  339.6 0.7 copy-start.15
  365.1 1.0 copy-start.2
  368.9 0.7 copy-start.13
  405.5 2.6 copy-start.9
  413.3 0.7 copy-start.16
  413.9 0.7 copy-start.7
  438.5 1.0 copy-start.4
  440.6 36.8 %copy-start.5 = (f32[512,128]{0,1:T(8,128)S(1)}, f32[512,128]{0,1:T(8,128)}, u32[]{:S(2)}) copy-start(f32[512,128]{0,1:T(8,128)} %copy-done.4) | copy-start | bytes 786436
Sparse Core Ops, SparseCore 0:
  10.5 48.2 all-reduce.3
  102.6 116.9 all-reduce.5
where the time goes:
time: 496 us; the launch traced here: 488 us
  other arithmetic  207 us (42%)
  waiting for transfers between devices  165 us (33%)
  matrix products  57 us (11%)
  local copies, waits for them, and re-layouts  29.2 us (6%)
  between operations  19.3 us (4%)
  blocking collectives  10.5 us (2%)
    psum x1, waiting for transfers between devices, shards(): gram = lax.psum(mm(joined_t, joined_t.T), 'pipe')  116 us
    another operation x14, other arithmetic, merged_coords(): lower = jnp.linalg.cholesky(mm_tn(image, mm(gram, image)))  69.8 us
    another operation x7, other arithmetic, solve_lower_t(): lax.linalg.triangular_solve(lower, block, left_side=False, lower=True, tr...  64.4 us
    psum x1, waiting for transfers between devices, shards(): both = lax.psum(jnp.concatenate([left_part, right_part], axis=1), 'tensor')  48.4 us
    another operation x7, other arithmetic, merged_coords(): lower = jnp.linalg.cholesky(mm_tn(weights, weights))  34.8 us
    another operation x6, other arithmetic, merged_coords(): lower = jnp.linalg.cholesky(mm_tn(pick, mm(gram, pick)))  34.4 us
    dot_general x1, matrix products, shards(): jnp.einsum('etk,etl->ekl', left_all, right_all, precision=lax.Precision.H...  16.5 us
    dot_general x8, matrix products, mm(): return jnp.matmul(a, b, precision=lax.Precision.HIGHEST)  14.7 us
  transfers between devices with their start and end apart: 2, of which 2 were waited for; matrix products, arithmetic and copies ran while one was open for 0% of the time, Pallas kernels for 0%

commit v1 on v0

--- a/solution.py
+++ b/solution.py
@@ -57,7 +57,7 @@
     right_all = both[:, width:].reshape(-1, TOK_EX, width)
     outer = jnp.einsum("etk,etl->ekl", left_all, right_all, precision=lax.Precision.HIGHEST)
     joined_t = outer.reshape(outer.shape[0], -1)
-    gram = lax.psum(mm(joined_t, joined_t.T), "pipe")
+    gram = jnp.sum(lax.all_gather(mm(joined_t, joined_t.T), "pipe"), axis=0)
     coords = merged_coords(gram)
     part_rows = joined_t.shape[1] // tensor_count
     rows = lax.dynamic_slice_in_dim(joined_t, tensor_pos * part_rows, part_rows, 1)

time: 496 us -> 487 us (0.982)
  waiting for transfers between devices: 165 us -> 148 us
  other arithmetic: 207 us -> 216 us
    psum x1 -> x0, waiting for transfers between devices: 116 us -> none  [shards(): gram = lax.psum(mm(joined_t, joined_t.T), 'pipe')]
    all_gather x0 -> x1, waiting for transfers between devices: none -> 99.7 us  [shards(): gram = jnp.sum(lax.all_gather(mm(joined_t, joined_t.T), 'pipe'), axis=0)]
    reduce_sum x0 -> x1, other arithmetic: none -> 7.91 us  [shards(): gram = jnp.sum(lax.all_gather(mm(joined_t, joined_t.T), 'pipe'), axis=0)]
where the time goes in v1:
time: 487 us; the launch traced here: 479 us
  other arithmetic  216 us (44%)
  waiting for transfers between devices  148 us (30%)
  matrix products  55.6 us (11%)
  local copies, waits for them, and re-layouts  29.4 us (6%)
  between operations  19.2 us (4%)
  blocking collectives  10.5 us (2%)
    all_gather x1, waiting for transfers between devices, shards(): gram = jnp.sum(lax.all_gather(mm(joined_t, joined_t.T), 'pipe'), axis=0)  99.7 us
    another operation x14, other arithmetic, merged_coords(): lower = jnp.linalg.cholesky(mm_tn(image, mm(gram, image)))  69.7 us
    another operation x7, other arithmetic, solve_lower_t(): lax.linalg.triangular_solve(lower, block, left_side=False, lower=True, tr...  64.9 us
    psum x1, waiting for transfers between devices, shards(): both = lax.psum(jnp.concatenate([left_part, right_part], axis=1), 'tensor')  48.4 us
    another operation x7, other arithmetic, merged_coords(): lower = jnp.linalg.cholesky(mm_tn(weights, weights))  34.8 us
    another operation x6, other arithmetic, merged_coords(): lower = jnp.linalg.cholesky(mm_tn(pick, mm(gram, pick)))  34.1 us
    dot_general x1, matrix products, shards(): jnp.einsum('etk,etl->ekl', left_all, right_all, precision=lax.Precision.H...  16.5 us
    dot_general x8, matrix products, mm(): return jnp.matmul(a, b, precision=lax.Precision.HIGHEST)  13.4 us
  transfers between devices with their start and end apart: 2, of which 2 were waited for; matrix products, arithmetic and copies ran while one was open for 0% of the time, Pallas kernels for 0%

profile of v1, /device:TPU:1, one launch (start us, length us, event | category | flops | bytes accessed | tf_op | source)
XLA Modules:
  0.0 479.0 jit_solution(6050604153519101934)
XLA Ops:
  6.5 1.4 convolution_convert_fusion
  10.4 48.4 %all-reduce.3.cloned.1.call-done = f32[512,64]{0,1:T(8,128)} async-done(((f32[512,64]{0,1:T(8,128)}), f32[512,64]{0,1:T(8,128)}) %all-reduce.3.cloned.1.call-update) | async-done | bytes 131088 | tf_op jit(solution)/shard_map/psum | solution.py:54
  58.8 10.5 %all_gather.9 = f32[2048,64]{0,1:T(8,128)S(1)} all-gather(f32[512,64]{0,1:T(8,128)} %all-reduce.3.cloned.1.call-done), channel_id=1, replica_groups=mesh['pipe'=16,'dp'=4,'tensor'=4] {'dp'}, dimensions={0}, use_global_device_ids=true | all-gather | bytes 655360 | tf_op jit(solution)/shard_map/all_gather | solution.py:55
  70.1 1.3 copy.15
  71.4 1.4 copy.16
  72.8 16.5 %fusion.90 = f32[512,32,32]{2,1,0:T(8,128)} fusion(f32[512,4,32]{2,1,0:T(4,128)S(1)} %bitcast.170, f32[512,4,32]{2,1,0:T(4,128)} %bitcast.171), kind=kOutput, calls=%fused_computation.147 | convolution fusion | flops 25165824 | bytes 2621440 | tf_op jit(solution)/shard_map/etk,etl->ekl/dot_general | solution.py:58
  89.2 6.4 %copy.17 = f32[512,32,32]{0,2,1:T(8,128)} copy(f32[512,32,32]{2,1,0:T(8,128)} %fusion.90) | data formatting | bytes 4194304 | tf_op jit(solution)/shard_map/etk,etl->ekl/dot_general | solution.py:58
  95.7 6.7 %convolution_bitcast_fusion = f32[512,512]{1,0:T(8,128)} fusion(f32[512,32,32]{0,2,1:T(8,128)} %copy.17), kind=kOutput, calls=%fused_computation.10 | convolution fusion | flops 3221225472 | bytes 3145728 | tf_op jit(solution)/shard_map/dot_general | solution.py:12
  103.3 99.7 %all-gather.3.cloned.1.call-done = f32[8192,512]{1,0:T(8,128)} async-done(((f32[512,512]{1,0:T(8,128)}), f32[8192,512]{1,0:T(8,128)}) %all-gather.3.cloned.1.call-update) | async-done | bytes 16777232 | tf_op jit(solution)/shard_map/all_gather | solution.py:60
  203.0 7.9 %reduce_sum.9 = f32[512,512]{1,0:T(8,128)S(1)} reduce(f32[16,512,512]{2,1,0:T(8,128)} %bitcast.169, f32[]{:T(128)} %constant.71.clone.1), dimensions={0}, to_apply=%region_1.0 | reduce | flops 3932160 | bytes 17825796 | tf_op jit(solution)/shard_map/reduce_sum | solution.py:60
  212.2 0.8 copy.20
  213.0 1.0 fusion.31
  214.7 11.7 %cholesky.214 = f32[128,128]{1,0:T(8,128)S(1)} custom-call(f32[128,128]{1,0:T(8,128)S(1)} %cholesky.346), custom_call_target="Cholesky" | custom-call | tf_op jit(solution)/shard_map/jit(cholesky)/cholesky | solution.py:27
  226.5 10.0 %custom-call.16 = f32[1,128,128]{1,2,0:T(8,128)S(1)} custom-call(f32[1,128,128]{2,1,0:T(8,128)S(1)} %get-tuple-element.79), custom_call_target="InvertDiagBlocksLowerTriangular" | custom-call | tf_op jit(solution)/shard_map/jit(cholesky)/cholesky | solution.py:27
  236.5 1.0 constant_dynamic-update-slice_fusion.7
  237.6 1.1 convolution_subtract_fusion.6
  238.7 11.7 %cholesky.231 = f32[128,128]{1,0:T(8,128)S(1)} custom-call(f32[128,128]{1,0:T(8,128)S(1)} %convolution_subtract_fusion.6), custom_call_target="Cholesky" | custom-call | tf_op jit(solution)/shard_map/jit(cholesky)/cholesky | solution.py:27
  252.3 1.0 select_select_fusion.2
  253.4 3.9 while.6
  254.0 1.3 bitcast_dynamic-update-slice_fusion.6
  256.0 1.3 bitcast_dynamic-update-slice_fusion.6
  257.9 20.9 %custom-call.17 = f32[2,128,128]{1,2,0:T(8,128)S(1)} custom-call(f32[2,128,128]{2,1,0:T(8,128)} %copy-done.13), custom_call_target="InvertDiagBlocksLowerTriangular" | custom-call | tf_op jit(solution)/shard_map/triangular_solve/custom-call.0 | solution.py:20
  278.9 1.4 fusion.26
  280.3 1.5 convolution_subtract_fusion.2
  282.2 1.0 fusion.10
  283.3 1.0 fusion.91
  284.3 1.0 fusion.92
  285.3 0.8 copy.21
  286.1 1.0 fusion.30
  287.8 11.7 %cholesky.248 = f32[128,128]{1,0:T(8,128)S(1)} custom-call(f32[128,128]{1,0:T(8,128)S(1)} %cholesky.349), custom_call_target="Cholesky" | custom-call | tf_op jit(solution)/shard_map/jit(cholesky)/cholesky | solution.py:31
  299.6 9.8 %custom-call.18 = f32[1,128,128]{1,2,0:T(8,128)S(1)} custom-call(f32[1,128,128]{2,1,0:T(8,128)S(1)} %get-tuple-element.75), custom_call_target="InvertDiagBlocksLowerTriangular" | custom-call | tf_op jit(solution)/shard_map/jit(cholesky)/cholesky | solution.py:31
  309.4 1.0 constant_dynamic-update-slice_fusion.5
  310.5 1.1 convolution_subtract_fusion.5
  311.6 11.9 %cholesky.265 = f32[128,128]{1,0:T(8,128)S(1)} custom-call(f32[128,128]{1,0:T(8,128)S(1)} %convolution_subtract_fusion.5), custom_call_target="Cholesky" | custom-call | tf_op jit(solution)/shard_map/jit(cholesky)/cholesky | solution.py:31
  326.1 1.0 select_select_fusion.1
  327.1 3.9 while.7
  327.7 1.3 bitcast_dynamic-update-slice_fusion.7
  329.6 1.3 bitcast_dynamic-update-slice_fusion.7
  331.7 20.5 %custom-call.19 = f32[2,128,128]{1,2,0:T(8,128)S(1)} custom-call(f32[2,128,128]{2,1,0:T(8,128)} %copy-done.14), custom_call_target="InvertDiagBlocksLowerTriangular" | custom-call | tf_op jit(solution)/shard_map/triangular_solve/custom-call.0 | solution.py:20
  352.1 1.4 fusion.24
  353.5 1.5 convolution_subtract_fusion.1
  355.5 1.0 fusion.14
  356.5 1.0 fusion.93
  357.5 1.0 fusion.94
  359.4 1.0 fusion.29
  361.1 11.7 %cholesky.282 = f32[128,128]{1,0:T(8,128)S(1)} custom-call(f32[128,128]{1,0:T(8,128)S(1)} %cholesky.352), custom_call_target="Cholesky" | custom-call | tf_op jit(solution)/shard_map/jit(cholesky)/cholesky | solution.py:31
  372.9 9.8 %custom-call.20 = f32[1,128,128]{1,2,0:T(8,128)S(1)} custom-call(f32[1,128,128]{2,1,0:T(8,128)S(1)} %get-tuple-element.71), custom_call_target="InvertDiagBlocksLowerTriangular" | custom-call | tf_op jit(solution)/shard_map/jit(cholesky)/cholesky | solution.py:31
  382.7 1.0 constant_dynamic-update-slice_fusion.2
  383.7 1.1 convolution_subtract_fusion.4
  384.8 12.1 %cholesky.299 = f32[128,128]{1,0:T(8,128)S(1)} custom-call(f32[128,128]{1,0:T(8,128)S(1)} %convolution_subtract_fusion.4), custom_call_target="Cholesky" | custom-call | tf_op jit(solution)/shard_map/jit(cholesky)/cholesky | solution.py:31
  399.5 1.0 select_select_fusion
  400.5 3.9 while.8
  401.1 1.3 bitcast_dynamic-update-slice_fusion.8
  403.1 1.3 bitcast_dynamic-update-slice_fusion.8
  405.8 20.5 %custom-call.21 = f32[2,128,128]{1,2,0:T(8,128)S(1)} custom-call(f32[2,128,128]{2,1,0:T(8,128)} %copy-done.15), custom_call_target="InvertDiagBlocksLowerTriangular" | custom-call | tf_op jit(solution)/shard_map/triangular_solve/custom-call.0 | solution.py:20
  426.3 1.4 fusion.22
  427.7 1.6 convolution_subtract_fusion
  429.7 1.0 fusion.21
  430.8 1.0 fusion.95
  432.0 11.7 %cholesky.316 = f32[128,128]{1,0:T(8,128)S(1)} custom-call(f32[128,128]{1,0:T(8,128)S(1)} %cholesky.355), custom_call_target="Cholesky" | custom-call | tf_op jit(solution)/shard_map/jit(cholesky)/cholesky | solution.py:34
  443.8 9.8 %custom-call.22 = f32[1,128,128]{1,2,0:T(8,128)S(1)} custom-call(f32[1,128,128]{2,1,0:T(8,128)S(1)} %get-tuple-element.67), custom_call_target="InvertDiagBlocksLowerTriangular" | custom-call | tf_op jit(solution)/shard_map/jit(cholesky)/cholesky | solution.py:34
  454.1 11.9 %cholesky.333 = f32[128,128]{1,0:T(8,128)S(1)} custom-call(f32[128,128]{1,0:T(8,128)S(1)} %convolution_subtract_fusion.3), custom_call_target="Cholesky" | custom-call | tf_op jit(solution)/shard_map/jit(cholesky)/cholesky | solution.py:34
  468.6 1.0 fusion.20
  469.6 2.4 fusion.18
  (94 shorter events, 21.4 us)
Async XLA Ops:
  6.5 1.7 copy-start
  6.5 52.3 %all-reduce.3.cloned.1.call-start = ((), (), s32[]{:S(2)}) async-start(), calls=%async_computation | async-start | bytes 262144 | tf_op jit(solution)/shard_map/psum | solution.py:54
  6.5 2.4 copy-start.5
  10.4 192.6 %all-gather.3.cloned.1.call-start = ((), (), s32[]{:S(2)}) async-start(), calls=%async_computation.1 | async-start | bytes 17825792 | tf_op jit(solution)/shard_map/all_gather | solution.py:60
  214.0 0.7 copy-start.10
  250.4 1.9 copy-start.9
  257.3 0.6 copy-start.13
  283.3 1.0 copy-start.2
  287.1 0.7 copy-start.11
  323.5 2.6 copy-start.7
  331.0 0.7 copy-start.14
  356.5 1.0 copy-start.1
  360.4 0.7 copy-start.12
  397.0 2.6 copy-start.8
  404.5 0.7 copy-start.15
  405.1 0.7 copy-start.6
  429.7 1.0 copy-start.3
  431.8 36.8 %copy-start.4 = (f32[512,128]{0,1:T(8,128)S(1)}, f32[512,128]{0,1:T(8,128)}, u32[]{:S(2)}) copy-start(f32[512,128]{0,1:T(8,128)} %copy-done.3) | copy-start | bytes 786436
Sparse Core Ops, SparseCore 0:
  10.5 48.2 all-reduce.2
  102.5 100.4 all-gather.2
